TPU v7x, 32 devices: a whole 2x2x4 slice. The times are simulated.
32 devices in a mesh: point: 8 (over y, x, core), batch: 4 (over z).
Axes of the slice: x: 2, y: 2, z: 4, core: 2. Of those that a mesh axis runs over, the one named last changes fastest.
Arguments:
- activations: bfloat16 [128, 14, 14, 1024], P('batch'), may hold values from -8 to 8
- labels: int32 [128], P('batch'), may hold values from 0 to 999
- t_values: float32 [64], replicated, may hold values from 0 to 1
- point_index: int32 [8], replicated, may hold values from 0 to 63
- w_reduce: bfloat16 [3, 1024, 256], P(None, 'point'), may hold values from -1 to 1
- w_spatial: bfloat16 [3, 2304, 256], P(None, 'point'), may hold values from -0.125 to 0.125
- w_expand: bfloat16 [3, 256, 1024], P(None, 'point'), may hold values from -0.375 to 0.375
- w_classes: bfloat16 [3, 1000, 1024], P(None, None, 'point'), may hold values from -0.1875 to 0.1875
- norm_gain: float32 [3, 1536], replicated, may hold values from 0.5 to 1.5
- norm_bias: float32 [3, 1536], replicated, may hold values from -3 to 3
- class_bias: float32 [3, 1000], replicated, may hold values from -3 to 3
Outputs:
- mean_reduce: float32 [8, 256], P('point')
- var_reduce: float32 [8, 256], P('point')
- mean_spatial: float32 [8, 256], P('point')
- var_spatial: float32 [8, 256], P('point')
- mean_expand: float32 [8, 1024], P('point')
- var_expand: float32 [8, 1024], P('point')
- margin: float32 [8], replicated
All inputs are finite; a program needn't handle non-finite values.
Results may differ from a plain program's by a relative error of at most 0.003.
Values may be sent and summed in bfloat16 or wider, within the bound.
A program may use at most 128 MiB of HBM per device.

v0:
```python
import jax
import jax.numpy as jnp
from jax import lax
from jax.sharding import PartitionSpec as P

EPSILON = 1e-05


def curve_coefficients(t_values, point_index):
    table_size = t_values.shape[0]
    matches = point_index[:, None] == jnp.arange(table_size, dtype=jnp.int32)[None, :]
    picked = jnp.sum(jnp.where(matches, t_values[None, :], 0.0), axis=1)
    doubled = 2.0 * picked
    return jnp.stack(
        [
            jnp.maximum(1.0 - doubled, 0.0),
            1.0 - jnp.abs(1.0 - doubled),
            jnp.maximum(doubled - 1.0, 0.0),
        ],
        axis=1,
    )


def blend_all(coefficients, endpoints):
    target_shape = (coefficients.shape[0],) + (1,) * (endpoints.ndim - 1)
    start_part = coefficients[:, 0].reshape(target_shape) * endpoints[0].astype(jnp.float32)[None]
    bend_part = coefficients[:, 1].reshape(target_shape) * endpoints[1].astype(jnp.float32)[None]
    final_part = coefficients[:, 2].reshape(target_shape) * endpoints[2].astype(jnp.float32)[None]
    return start_part + bend_part + final_part


def point_weight(endpoints, own_row, by_columns):
    if by_columns:
        gathered = lax.all_gather(endpoints, "point", axis=2, tiled=True)
    else:
        gathered = lax.all_gather(endpoints, "point", axis=1, tiled=True)
    return blend_all(own_row, gathered)[0].astype(jnp.bfloat16)


def map_product(maps, kernel):
    return lax.dot_general(
        maps, kernel, (((3,), (0,)), ((), ())), preferred_element_type=jnp.float32
    )


def batch_norm(pre_norm, gain_part, bias_part, row_count):
    channel_total, channel_squares = lax.psum(
        (jnp.sum(pre_norm, axis=(0, 1, 2)), jnp.sum(pre_norm * pre_norm, axis=(0, 1, 2))), "batch"
    )
    channel_mean = channel_total / row_count
    channel_var = channel_squares / row_count - channel_mean * channel_mean
    scaled = (pre_norm - channel_mean) * lax.rsqrt(channel_var + EPSILON) * gain_part + bias_part
    return (channel_mean, channel_var, scaled)


def spatial_conv(source, kernel):
    side_len = source.shape[1]
    middle = source.shape[3]
    padded = jnp.pad(source, ((0, 0), (1, 1), (1, 1), (0, 0)))
    widened = jnp.concatenate(
        [
            padded[:, :, 0:side_len, :],
            padded[:, :, 1 : side_len + 1, :],
            padded[:, :, 2 : side_len + 2, :],
        ],
        axis=3,
    )
    summed = map_product(widened[:, 0:side_len], kernel[0 : 3 * middle])
    summed = summed + map_product(widened[:, 1 : side_len + 1], kernel[3 * middle : 6 * middle])
    summed = summed + map_product(widened[:, 2 : side_len + 2], kernel[6 * middle : 9 * middle])
    return summed


def shards(
    activations,
    labels,
    t_values,
    point_index,
    w_reduce,
    w_spatial,
    w_expand,
    w_classes,
    norm_gain,
    norm_bias,
    class_bias,
):
    coefficients = curve_coefficients(t_values, point_index)
    own_row = lax.dynamic_slice_in_dim(coefficients, lax.axis_index("point"), 1, 0)
    reduce_w = point_weight(w_reduce, own_row, False)
    spatial_w = point_weight(w_spatial, own_row, False)
    expand_w = point_weight(w_expand, own_row, False)
    class_w = point_weight(w_classes, own_row, True)
    gain_now = blend_all(own_row, norm_gain)[0]
    bias_now = blend_all(own_row, norm_bias)[0]
    shift_now = blend_all(own_row, class_bias)[0]
    images, side_len, _, channels = activations.shape
    middle = w_reduce.shape[2]
    row_count = float(images * side_len * side_len * lax.axis_size("batch"))
    reduced = map_product(activations, reduce_w)
    mean_one, var_one, normed_one = batch_norm(
        reduced, gain_now[:middle], bias_now[:middle], row_count
    )
    first = jax.nn.relu(normed_one).astype(jnp.bfloat16)
    spatial = spatial_conv(first, spatial_w)
    mean_two, var_two, normed_two = batch_norm(
        spatial, gain_now[middle : 2 * middle], bias_now[middle : 2 * middle], row_count
    )
    second = jax.nn.relu(normed_two).astype(jnp.bfloat16)
    expanded = map_product(second, expand_w)
    mean_three, var_three, normed_three = batch_norm(
        expanded, gain_now[2 * middle :], bias_now[2 * middle :], row_count
    )
    block_out = jax.nn.relu(normed_three + activations.astype(jnp.float32))
    pooled = jnp.mean(block_out, axis=(1, 2)).astype(jnp.bfloat16)
    logits = (
        lax.dot_general(
            pooled, class_w, (((1,), (1,)), ((), ())), preferred_element_type=jnp.float32
        )
        + shift_now
    )
    classes = logits.shape[1]
    onehot = labels[:, None] == jnp.arange(classes, dtype=jnp.int32)[None, :]
    correct = jnp.sum(jnp.where(onehot, logits, 0.0), axis=1)
    rivals = jnp.max(jnp.where(onehot, -1e30, logits), axis=1)
    partial_value = jnp.sum(correct - rivals) / (images * lax.axis_size("batch"))
    point_count = point_index.shape[0]
    placed = jnp.where(
        jnp.arange(point_count, dtype=jnp.int32) == lax.axis_index("point"), partial_value, 0.0
    )
    margin_all = lax.psum(placed, ("point", "batch"))
    return (
        mean_one[None],
        var_one[None],
        mean_two[None],
        var_two[None],
        mean_three[None],
        var_three[None],
        margin_all,
    )


def solution(mesh):
    placed = (
        P("batch", None, None, None),
        P("batch"),
        P(),
        P(),
        P(None, "point", None),
        P(None, "point", None),
        P(None, "point", None),
        P(None, None, "point"),
        P(),
        P(),
        P(),
    )
    return jax.shard_map(
        shards,
        mesh=mesh,
        in_specs=placed,
        out_specs=(
            P("point", None),
            P("point", None),
            P("point", None),
            P("point", None),
            P("point", None),
            P("point", None),
            P(),
        ),
        check_vma=False,
    )
```

profile of v0, /device:TPU:0, one launch (start us, length us, event | category | flops | bytes accessed | tf_op | source)
XLA Modules:
  0.0 208.5 jit_solution(10090536275269189656)
XLA Ops:
  7.2 0.7 all-gather.5.cloned.1.call-update
  7.9 0.7 all-gather.7.cloned.1.call-update
  8.7 0.7 all-gather.9.cloned.1.call-update
  10.0 0.9 select_reduce_fusion.2
  11.5 2.8 %multiply_add_fusion = (f32[1,1536]{1,0:T(1,128)S(1)}, f32[1,1536]{1,0:T(1,128)S(1)}) fusion(f32[3,1536]{1,0:T(4,128)} %param.20, f32[]{:T(128)} %bitcast.5, f32[]{:T(128)} %bitcast.4, f32[]{:T(128)} %bitcast.3, f32[3,1536]{1,0:T(4,128)} %param.19), kind=kLoop, calls=%fused_computation.50 | loop fusion | flops 15360 | bytes 49164 | tf_op jit(solution)/shard_map/add | solution.py:29
  14.3 2.7 %multiply_add_fusion.2 = f32[1,1000]{1,0:T(1,128)S(1)} fusion(f32[3,1000]{1,0:T(4,128)} %param.21, f32[]{:T(128)} %bitcast.5, f32[]{:T(128)} %bitcast.4, f32[]{:T(128)} %bitcast.3), kind=kLoop, calls=%fused_computation.52 | loop fusion | flops 5000 | bytes 16012 | tf_op jit(solution)/shard_map/add | solution.py:29
  17.0 21.2 %all-gather.5.cloned.1.call-done = bf16[3,1024,256]{2,1,0:T(8,128)(2,1)} async-done(((bf16[3,128,256]{2,1,0:T(8,128)(2,1)}), bf16[3,1024,256]{2,1,0:T(8,128)(2,1)}) %all-gather.5.cloned.1.call-update) | async-done | bytes 1572880 | tf_op jit(solution)/shard_map/all_gather | solution.py:36
  38.2 13.3 %multiply_reduce_fusion.2 = (f32[256]{0:T(256)S(1)}, f32[256]{0:T(256)S(1)}, f32[256,32,14,14]{0,1,3,2:T(8,128)}) fusion(bf16[32,14,14,1024]{3,0,2,1:T(8,128)(2,1)} %param.11, bf16[3,1024,256]{2,1,0:T(8,128)(2,1)} %all-gather.5.cloned.1.call-done, f32[]{:T(128)} %bitcast.5, f32[]{:T(128)} %bitcast.4, f32[]{:T(128)} %bitcast.3), kind=kOutput, calls=%fused_computation.7 | convolution fusion | flops 3295510016 | bytes 20842508 | tf_op jit(solution)/shard_map/dot_general | solution.py:41
  51.5 11.7 %all-reduce.3 = (f32[256]{0:T(256)S(1)}, f32[256]{0:T(256)S(1)}) all-reduce(f32[256]{0:T(256)S(1)} %get-tuple-element.12, f32[256]{0:T(256)S(1)} %get-tuple-element.11), channel_id=1, replica_groups=mesh['point'=8,'batch'=4] {'batch'}, use_global_device_ids=true, to_apply=%region_2.3 | all-reduce | flops 512 | bytes 4096 | tf_op jit(solution)/shard_map/psum | solution.py:47
  63.8 4.1 %fusion.1 = bf16[32,14,14,256]{3,0,2,1:T(8,128)(2,1)S(1)} fusion(f32[256,32,14,14]{0,1,3,2:T(8,128)} %get-tuple-element.43, f32[256]{0:T(256)S(1)} %bitcast.77, f32[256]{0:T(256)S(1)} %bitcast.78, f32[256]{0:T(256)S(1)} %get-tuple-element.25, f32[256]{0:T(256)S(1)} %get-tuple-element.39), kind=kLoop, calls=%fused_computation.13 | loop fusion | flops 9633792 | bytes 9637888 | tf_op jit(solution)/shard_map/convert_element_type | solution.py:103
  67.9 4.9 %pad_slice_fusion.2 = (bf16[32,16,14,256]{3,0,2,1:T(8,128)(2,1)}, bf16[32,16,14,256]{3,0,2,1:T(8,128)(2,1)}, bf16[32,16,14,256]{3,0,2,1:T(8,128)(2,1)}) fusion(bf16[32,14,14,256]{3,0,2,1:T(8,128)(2,1)S(1)} %fusion.1), kind=kLoop, calls=%fused_computation.10 | loop fusion | bytes 14221312 | tf_op jit(solution)/shard_map/slice | solution.py:62
  72.8 1.2 all-gather.7.cloned.1.call-done
  74.0 4.5 %add_convert_fusion.1 = bf16[1,2304,256]{2,1,0:T(8,128)(2,1)S(1)} fusion(bf16[3,2304,256]{2,1,0:T(8,128)(2,1)} %all-gather.7.cloned.1.call-done, f32[]{:T(128)} %bitcast.5, f32[]{:T(128)} %bitcast.4, f32[]{:T(128)} %bitcast.3), kind=kLoop, calls=%fused_computation.19 | loop fusion | flops 5308416 | bytes 4718604 | tf_op jit(solution)/shard_map/convert_element_type | solution.py:37
  78.5 7.3 %fusion.31 = f32[32,14,14,256]{3,0,2,1:T(8,128)} fusion(bf16[1,2304,256]{2,1,0:T(8,128)(2,1)S(1)} %add_convert_fusion.1, bf16[32,16,14,256]{3,0,2,1:T(8,128)(2,1)} %get-tuple-element.29, bf16[32,16,14,256]{3,0,2,1:T(8,128)(2,1)} %get-tuple-element.28, bf16[32,16,14,256]{3,0,2,1:T(8,128)(2,1)} %get-tuple-element.27), kind=kOutput, calls=%fused_computation.44 | convolution fusion | flops 2499280896 | bytes 17825792 | tf_op jit(solution)/shard_map/dot_general | solution.py:41
  85.8 1.2 copy-done.1
  87.0 1.0 copy-done.2
  88.0 5.4 %fusion.30 = f32[32,14,14,256]{3,0,2,1:T(8,128)} fusion(bf16[1,2304,256]{2,1,0:T(8,128)(2,1)S(1)} %add_convert_fusion.1, bf16[32,16,14,256]{3,0,2,1:T(8,128)(2,1)S(1)} %copy-done.2, bf16[32,16,14,256]{3,0,2,1:T(8,128)(2,1)S(1)} %copy-done.1, bf16[32,16,14,256]{3,0,2,1:T(8,128)(2,1)S(1)} %copy-done), kind=kOutput, calls=%fused_computation.42 | convolution fusion | flops 2499280896 | bytes 17825792 | tf_op jit(solution)/shard_map/dot_general | solution.py:41
  93.4 9.0 %multiply_reduce_fusion.1 = (f32[256]{0:T(256)S(1)}, f32[256]{0:T(256)S(1)}, f32[32,14,14,256]{3,0,2,1:T(8,128)}) fusion(bf16[1,2304,256]{2,1,0:T(8,128)(2,1)S(1)} %add_convert_fusion.1, bf16[32,16,14,256]{3,0,2,1:T(8,128)(2,1)S(1)} %copy-done.2, bf16[32,16,14,256]{3,0,2,1:T(8,128)(2,1)S(1)} %copy-done.1, bf16[32,16,14,256]{3,0,2,1:T(8,128)(2,1)S(1)} %copy-done, ...), kind=kOutput, calls=%fused_computation.5 | convolution fusion | flops 2507308544 | bytes 30672896 | tf_op jit(solution)/shard_map/dot_general | solution.py:41
  102.4 11.9 %all-reduce.2 = (f32[256]{0:T(256)S(1)}, f32[256]{0:T(256)S(1)}) all-reduce(f32[256]{0:T(256)S(1)} %get-tuple-element.10, f32[256]{0:T(256)S(1)} %get-tuple-element.9), channel_id=1, replica_groups=mesh['point'=8,'batch'=4] {'batch'}, use_global_device_ids=true, to_apply=%region_6.7 | all-reduce | flops 512 | bytes 4096 | tf_op jit(solution)/shard_map/psum | solution.py:47
  114.9 16.0 %multiply_reduce_fusion = (f32[1024]{0:T(1024)S(1)}, f32[1024]{0:T(1024)S(1)}, f32[32,14,14,1024]{3,0,2,1:T(8,128)}) fusion(bf16[3,256,1024]{2,1,0:T(8,128)(2,1)} %all-gather.9.cloned.1.call-done, f32[]{:T(128)} %bitcast.5, f32[]{:T(128)} %bitcast.4, f32[]{:T(128)} %bitcast.3, f32[32,14,14,256]{3,0,2,1:T(8,128)} %get-tuple-element.44, f32[256]{0:T(256)S(1)} %bitcast.84, ...), kind=kOutput, calls=%fused_computation.1 | convolution fusion | flops 3319592960 | bytes 33697804 | tf_op jit(solution)/shard_map/dot_general | solution.py:41
  130.9 8.5 %all-reduce.1 = (f32[1024]{0:T(1024)S(1)}, f32[1024]{0:T(1024)S(1)}) all-reduce(f32[1024]{0:T(1024)S(1)} %get-tuple-element.8, f32[1024]{0:T(1024)S(1)} %get-tuple-element.7), channel_id=1, replica_groups=mesh['point'=8,'batch'=4] {'batch'}, use_global_device_ids=true, to_apply=%region_10.11 | all-reduce | flops 2048 | bytes 16384 | tf_op jit(solution)/shard_map/psum | solution.py:47
  140.1 14.9 %maximum_reduce_fusion = f32[32,1024]{1,0:T(8,128)S(1)} fusion(bf16[32,14,14,1024]{3,0,2,1:T(8,128)(2,1)} %param.11, f32[32,14,14,1024]{3,0,2,1:T(8,128)} %get-tuple-element.45, f32[1024]{0:T(1024)S(1)} %bitcast.74, f32[1024]{0:T(1024)S(1)} %bitcast.75, f32[1024]{0:T(1024)S(1)} %get-tuple-element.21, f32[1024]{0:T(1024)S(1)} %get-tuple-element.34), kind=kLoop, calls=%fused_computation | loop fusion | flops 51347456 | bytes 38682624 | tf_op jit(solution)/shard_map/reduce_sum | solution.py:114
  155.0 6.1 %select_reduce_fusion = (f32[32]{0:T(128)S(1)}, f32[32]{0:T(128)S(1)}) fusion(s32[32]{0:T(128)S(1)} %copy-done.6, f32[1000]{0:T(1024)S(1)} %bitcast.80, bf16[3,1000,1024]{2,1,0:T(8,128)(2,1)} %all-gather.11.cloned.1.call-done, f32[]{:T(128)} %bitcast.5, f32[]{:T(128)} %bitcast.4, f32[]{:T(128)} %bitcast.3, f32[32,1024]{1,0:T(8,128)S(1)} %maximum_reduce_fusion), kind=kOutput, calls=%fused_computation.45 | convolution fusion | flops 75009472 | bytes 6279468 | tf_op jit(solution)/shard_map/dot_general | solution.py:116
  162.4 39.6 %psum.55 = f32[8]{0:T(128)} all-reduce(f32[8]{0:T(128)S(1)} %compare_select_fusion), channel_id=1, replica_groups=mesh['point'=8,'batch'=4] {'point','batch'}, use_global_device_ids=true, to_apply=%region_17.18 | all-reduce | flops 8 | bytes 64 | tf_op jit(solution)/shard_map/psum | solution.py:130
  (32 shorter events, 3.7 us)
Async XLA Ops:
  7.2 31.0 %all-gather.5.cloned.1.call-start = ((), (), s32[]{:S(2)}) async-start(), calls=%async_computation | async-start | bytes 1769472 | tf_op jit(solution)/shard_map/all_gather | solution.py:36
  7.9 66.1 %all-gather.7.cloned.1.call-start = ((), (), s32[]{:S(2)}) async-start(), calls=%async_computation.1 | async-start | bytes 3981312 | tf_op jit(solution)/shard_map/all_gather | solution.py:36
  8.7 106.3 %all-gather.9.cloned.1.call-start = ((), (), s32[]{:S(2)}) async-start(), calls=%async_computation.2 | async-start | bytes 1769472 | tf_op jit(solution)/shard_map/all_gather | solution.py:36
  9.4 145.6 %all-gather.11.cloned.1.call-start = ((), (), s32[]{:S(2)}) async-start(), calls=%async_computation.3 | async-start | bytes 6912000 | tf_op jit(solution)/shard_map/all_gather | solution.py:34
  63.8 9.0 %copy-start.4 = (f32[256]{0:T(256)}, f32[256]{0:T(256)S(1)}, u32[]{:S(2)}) copy-start(f32[256]{0:T(256)S(1)} %get-tuple-element.39) | copy-start | bytes 3076
  78.5 7.3 %copy-start = (bf16[32,16,14,256]{3,0,2,1:T(8,128)(2,1)S(1)}, bf16[32,16,14,256]{3,0,2,1:T(8,128)(2,1)}, u32[]{:S(2)}) copy-start(bf16[32,16,14,256]{3,0,2,1:T(8,128)(2,1)} %get-tuple-element.27) | copy-start | bytes 11010052
  78.5 8.5 %copy-start.1 = (bf16[32,16,14,256]{3,0,2,1:T(8,128)(2,1)S(1)}, bf16[32,16,14,256]{3,0,2,1:T(8,128)(2,1)}, u32[]{:S(2)}) copy-start(bf16[32,16,14,256]{3,0,2,1:T(8,128)(2,1)} %get-tuple-element.28) | copy-start | bytes 11010052
  78.5 9.5 %copy-start.2 = (bf16[32,16,14,256]{3,0,2,1:T(8,128)(2,1)S(1)}, bf16[32,16,14,256]{3,0,2,1:T(8,128)(2,1)}, u32[]{:S(2)}) copy-start(bf16[32,16,14,256]{3,0,2,1:T(8,128)(2,1)} %get-tuple-element.29) | copy-start | bytes 11010052
  114.9 16.0 %copy-start.5 = (f32[256]{0:T(256)}, f32[256]{0:T(256)S(1)}, u32[]{:S(2)}) copy-start(f32[256]{0:T(256)S(1)} %get-tuple-element.38) | copy-start | bytes 3076
  140.1 14.9 %copy-start.3 = (f32[1024]{0:T(1024)}, f32[1024]{0:T(1024)S(1)}, u32[]{:S(2)}) copy-start(f32[1024]{0:T(1024)S(1)} %get-tuple-element.34) | copy-start | bytes 12292
  140.1 14.9 %copy-start.6 = (s32[32]{0:T(128)S(1)}, s32[32]{0:T(128)}, u32[]{:S(2)}) copy-start(s32[32]{0:T(128)} %param.12) | copy-start | bytes 388
Sparse Core Ops, SparseCore 0:
  9.9 28.2 all-gather.4
  40.1 33.8 all-gather.6
  75.9 25.5 all-gather.8
  103.2 45.9 all-gather.10
where the time goes:
time: 209 us; the launch traced here: 208 us
  blocking collectives  71.7 us (34%)
  matrix products  57.1 us (27%)
  other arithmetic  32.2 us (15%)
  waiting for transfers between devices  24.9 us (12%)
  between operations  14.6 us (7%)
  local copies, waits for them, and re-layouts  7.82 us (4%)
    dot_general x5, matrix products, map_product(): lax.dot_general(maps, kernel, (((3,), (0,)), ((), ())), preferred_element...  51 us
    psum x1, blocking collectives, shards(): margin_all = lax.psum(placed, ('point', 'batch'))  39.6 us
    psum x3, blocking collectives, batch_norm(): lax.psum((jnp.sum(pre_norm, axis=(0, 1, 2)), jnp.sum(pre_norm * pre_norm,...  32.1 us
    all_gather x3, waiting for transfers between devices, point_weight(): gathered = lax.all_gather(endpoints, 'point', axis=1, tiled=True)  22.3 us
    reduce_sum x1, other arithmetic, shards(): pooled = jnp.mean(block_out, axis=(1, 2)).astype(jnp.bfloat16)  14.9 us
    dot_general x1, matrix products, shards(): lax.dot_general(pooled, class_w, (((1,), (1,)), ((), ())), preferred_elem...  6.09 us
    add x2, other arithmetic, blend_all(): return start_part + bend_part + final_part  5.52 us
    slice x1, local copies, waits for them, and re-layouts, spatial_conv(): padded[:, :, 0:side_len, :]  4.94 us
  transfers between devices with their start and end apart: 4, of which 2 were waited for; matrix products, arithmetic and copies ran while one was open for 42% of the time, Pallas kernels for 0%

commit v1 on v0

--- a/solution.py
+++ b/solution.py
@@ -33,7 +33,7 @@
     if by_columns:
         gathered = lax.all_gather(endpoints, "point", axis=2, tiled=True)
     else:
-        gathered = lax.all_gather(endpoints, "point", axis=1, tiled=True)
+        gathered = jnp.concatenate(lax.all_gather(endpoints, "point"), axis=1)
     return blend_all(own_row, gathered)[0].astype(jnp.bfloat16)
 
 

time: 209 us -> 232 us (1.11)
  waiting for transfers between devices: 24.9 us -> 47.7 us
  matrix products: 57.1 us -> 50.5 us
  other arithmetic: 32.2 us -> 38.5 us
    all_gather x3, waiting for transfers between devices: 22.3 us -> 45.1 us  [point_weight(): gathered = jnp.concatenate(lax.all_gather(endpoints, 'point'), axis=1)]
    another operation x0 -> x3, other arithmetic: none -> 11 us
    dot_general x5, matrix products: 51 us -> 44.4 us  [map_product(): lax.dot_general(maps, kernel, (((3,), (0,)), ((), ())), preferred_element...]
    convert_element_type x1 -> x0, other arithmetic: 4.52 us -> none  [point_weight(): return blend_all(own_row, gathered)[0].astype(jnp.bfloat16)]
    all_gather x0 -> x1, local copies, waits for them, and re-layouts: none -> 2.39 us  [point_weight(): gathered = jnp.concatenate(lax.all_gather(endpoints, 'point'), axis=1)]
  transfers between devices with their start and end apart: 4 -> 4, of which waited for: 2 -> 3; matrix products, arithmetic and copies ran while one was open for 42% -> 39% of each run, Pallas kernels for 0% -> 0%
where the time goes in v1:
time: 232 us; the launch traced here: 231 us
  blocking collectives  71.6 us (31%)
  matrix products  50.5 us (22%)
  waiting for transfers between devices  47.7 us (21%)
  other arithmetic  38.5 us (17%)
  between operations  14.6 us (6%)
  local copies, waits for them, and re-layouts  8 us (3%)
    all_gather x3, waiting for transfers between devices, point_weight(): gathered = jnp.concatenate(lax.all_gather(endpoints, 'point'), axis=1)  45.1 us
    dot_general x5, matrix products, map_product(): lax.dot_general(maps, kernel, (((3,), (0,)), ((), ())), preferred_element...  44.4 us
    psum x1, blocking collectives, shards(): margin_all = lax.psum(placed, ('point', 'batch'))  39.5 us
    psum x3, blocking collectives, batch_norm(): lax.psum((jnp.sum(pre_norm, axis=(0, 1, 2)), jnp.sum(pre_norm * pre_norm,...  32.1 us
    reduce_sum x1, other arithmetic, shards(): pooled = jnp.mean(block_out, axis=(1, 2)).astype(jnp.bfloat16)  14.7 us
    another operation x3, other arithmetic  11 us
    dot_general x1, matrix products, shards(): lax.dot_general(pooled, class_w, (((1,), (1,)), ((), ())), preferred_elem...  6.11 us
    add x2, other arithmetic, blend_all(): return start_part + bend_part + final_part  5.56 us
  transfers between devices with their start and end apart: 4, of which 3 were waited for; matrix products, arithmetic and copies ran while one was open for 39% of the time, Pallas kernels for 0%

profile of v1, /device:TPU:0, one launch (start us, length us, event | category | flops | bytes accessed | tf_op | source)
XLA Modules:
  0.0 231.1 jit_solution(203467350426466594)
XLA Ops:
  7.9 0.7 all-gather.14.cloned.1.call-update
  10.0 0.9 select_reduce_fusion.2
  11.5 2.8 %multiply_add_fusion = (f32[1,1536]{1,0:T(1,128)S(1)}, f32[1,1536]{1,0:T(1,128)S(1)}) fusion(f32[3,1536]{1,0:T(4,128)} %param.20, f32[]{:T(128)} %bitcast.8, f32[]{:T(128)} %bitcast.6, f32[]{:T(128)} %bitcast.3, f32[3,1536]{1,0:T(4,128)} %param.19), kind=kLoop, calls=%fused_computation.36 | loop fusion | flops 15360 | bytes 49164 | tf_op jit(solution)/shard_map/add | solution.py:29
  14.3 2.8 %multiply_add_fusion.2 = f32[1,1000]{1,0:T(1,128)S(1)} fusion(f32[3,1000]{1,0:T(4,128)} %param.21, f32[]{:T(128)} %bitcast.8, f32[]{:T(128)} %bitcast.6, f32[]{:T(128)} %bitcast.3), kind=kLoop, calls=%fused_computation.38 | loop fusion | flops 5000 | bytes 16012 | tf_op jit(solution)/shard_map/add | solution.py:29
  17.1 21.1 %all-gather.10.cloned.1.call-done = bf16[24,128,256]{2,1,0:T(8,128)(2,1)} async-done(((bf16[3,128,256]{2,1,0:T(8,128)(2,1)}), bf16[24,128,256]{2,1,0:T(8,128)(2,1)}) %all-gather.10.cloned.1.call-update) | async-done | bytes 1572880 | tf_op jit(solution)/shard_map/all_gather | solution.py:36
  38.2 3.6 %add_convert_fusion.3 = bf16[1,8,128,256]{3,2,0,1:T(8,128)(2,1)S(1)} fusion(bf16[3,8,128,256]{3,2,0,1:T(8,128)(2,1)} %bitcast.75, f32[]{:T(128)} %bitcast.8, f32[]{:T(128)} %bitcast.6, f32[]{:T(128)} %bitcast.3), kind=kLoop, calls=%fused_computation.25 | loop fusion | flops 2359296 | bytes 2097164 | tf_op jit(solution)/shard_map/convert.2
  41.8 10.8 %multiply_reduce_fusion.2 = (f32[256]{0:T(256)S(1)}, f32[256]{0:T(256)S(1)}, f32[256,32,14,14]{0,1,3,2:T(8,128)}) fusion(bf16[1024,256,1,1]{1,0,3,2:T(8,128)(2,1)S(1)} %bitcast.80, bf16[32,14,14,1024]{3,0,2,1:T(8,128)(2,1)} %param.11), kind=kOutput, calls=%fused_computation.7 | convolution fusion | flops 3293150720 | bytes 19793920 | tf_op jit(solution)/shard_map/dot_general | solution.py:41
  52.6 11.7 %all-reduce.3 = (f32[256]{0:T(256)S(1)}, f32[256]{0:T(256)S(1)}) all-reduce(f32[256]{0:T(256)S(1)} %get-tuple-element.12, f32[256]{0:T(256)S(1)} %get-tuple-element.11), channel_id=1, replica_groups=mesh['point'=8,'batch'=4] {'batch'}, use_global_device_ids=true, to_apply=%region_2.3 | all-reduce | flops 512 | bytes 4096 | tf_op jit(solution)/shard_map/psum | solution.py:47
  64.8 0.8 all-gather.14.cloned.1.call-done
  65.7 3.6 %add_convert_fusion.2 = bf16[1,8,32,1024]{3,2,0,1:T(8,128)(2,1)S(1)} fusion(bf16[3,8,32,1024]{3,2,0,1:T(8,128)(2,1)} %bitcast.74, f32[]{:T(128)} %bitcast.8, f32[]{:T(128)} %bitcast.6, f32[]{:T(128)} %bitcast.3), kind=kLoop, calls=%fused_computation.24 | loop fusion | flops 2359296 | bytes 2097164 | tf_op jit(solution)/shard_map/convert
  69.3 4.1 %fusion.1 = bf16[32,14,14,256]{3,0,2,1:T(8,128)(2,1)S(1)} fusion(f32[256,32,14,14]{0,1,3,2:T(8,128)} %get-tuple-element.43, f32[256]{0:T(256)S(1)} %bitcast.85, f32[256]{0:T(256)S(1)} %bitcast.86, f32[256]{0:T(256)S(1)} %get-tuple-element.25, f32[256]{0:T(256)S(1)} %get-tuple-element.39), kind=kLoop, calls=%fused_computation.14 | loop fusion | flops 9633792 | bytes 9637888 | tf_op jit(solution)/shard_map/convert_element_type | solution.py:103
  73.3 4.9 %pad_slice_fusion.2 = (bf16[32,16,14,256]{3,0,2,1:T(8,128)(2,1)}, bf16[32,16,14,256]{3,0,2,1:T(8,128)(2,1)}, bf16[32,16,14,256]{3,0,2,1:T(8,128)(2,1)}) fusion(bf16[32,14,14,256]{3,0,2,1:T(8,128)(2,1)S(1)} %fusion.1), kind=kLoop, calls=%fused_computation.10 | loop fusion | bytes 14221312 | tf_op jit(solution)/shard_map/slice | solution.py:62
  78.3 23.2 %all-gather.12.cloned.1.call-done = bf16[24,288,256]{2,1,0:T(8,128)(2,1)} async-done(((bf16[3,288,256]{2,1,0:T(8,128)(2,1)}), bf16[24,288,256]{2,1,0:T(8,128)(2,1)}) %all-gather.12.cloned.1.call-update) | async-done | bytes 3538960 | tf_op jit(solution)/shard_map/all_gather | solution.py:36
  101.4 2.4 %copy.27 = bf16[8,3,288,256]{3,2,0,1:T(8,128)(2,1)S(1)} copy(bf16[8,3,288,256]{3,2,1,0:T(8,128)(2,1)} %bitcast.73) | data formatting | bytes 7077888 | tf_op jit(solution)/shard_map/all_gather | solution.py:36
  103.8 3.8 %add_convert_fusion.1 = bf16[1,8,288,256]{3,2,1,0:T(8,128)(2,1)S(1)} fusion(bf16[3,8,288,256]{3,2,1,0:T(8,128)(2,1)S(1)} %bitcast.72, f32[]{:T(128)} %bitcast.8, f32[]{:T(128)} %bitcast.6, f32[]{:T(128)} %bitcast.3), kind=kLoop, calls=%fused_computation.20 | loop fusion | flops 5308416 | bytes 4718604 | tf_op jit(solution)/shard_map/convert.1
  107.7 5.3 %fusion.14 = f32[32,14,14,256]{3,0,2,1:T(8,128)} fusion(bf16[2304,256]{1,0:T(8,128)(2,1)S(1)} %bitcast.76, bf16[32,16,14,256]{3,0,2,1:T(8,128)(2,1)S(1)} %copy-done.2, bf16[32,16,14,256]{3,0,2,1:T(8,128)(2,1)S(1)} %copy-done.1, bf16[32,16,14,256]{3,0,2,1:T(8,128)(2,1)S(1)} %copy-done), kind=kOutput, calls=%fused_computation.30 | convolution fusion | flops 2499280896 | bytes 17825792 | tf_op jit(solution)/shard_map/dot_general | solution.py:41
  113.0 5.4 %fusion.13 = f32[32,14,14,256]{3,0,2,1:T(8,128)} fusion(bf16[2304,256]{1,0:T(8,128)(2,1)S(1)} %bitcast.77, bf16[32,16,14,256]{3,0,2,1:T(8,128)(2,1)S(1)} %copy-done.2, bf16[32,16,14,256]{3,0,2,1:T(8,128)(2,1)S(1)} %copy-done.1, bf16[32,16,14,256]{3,0,2,1:T(8,128)(2,1)S(1)} %copy-done), kind=kOutput, calls=%fused_computation.28 | convolution fusion | flops 2499280896 | bytes 17825792 | tf_op jit(solution)/shard_map/dot_general | solution.py:41
  118.3 8.9 %multiply_reduce_fusion.1 = (f32[256]{0:T(256)S(1)}, f32[256]{0:T(256)S(1)}, f32[32,14,14,256]{3,0,2,1:T(8,128)}) fusion(bf16[2304,256]{1,0:T(8,128)(2,1)S(1)} %bitcast.78, bf16[32,16,14,256]{3,0,2,1:T(8,128)(2,1)S(1)} %copy-done.2, bf16[32,16,14,256]{3,0,2,1:T(8,128)(2,1)S(1)} %copy-done.1, bf16[32,16,14,256]{3,0,2,1:T(8,128)(2,1)S(1)} %copy-done, ...), kind=kOutput, calls=%fused_computation.5 | convolution fusion | flops 2507308544 | bytes 30672896 | tf_op jit(solution)/shard_map/dot_general | solution.py:41
  127.3 11.8 %all-reduce.2 = (f32[256]{0:T(256)S(1)}, f32[256]{0:T(256)S(1)}) all-reduce(f32[256]{0:T(256)S(1)} %get-tuple-element.10, f32[256]{0:T(256)S(1)} %get-tuple-element.9), channel_id=1, replica_groups=mesh['point'=8,'batch'=4] {'batch'}, use_global_device_ids=true, to_apply=%region_6.7 | all-reduce | flops 512 | bytes 4096 | tf_op jit(solution)/shard_map/psum | solution.py:47
  139.7 14.0 %multiply_reduce_fusion = (f32[1024]{0:T(1024)S(1)}, f32[1024]{0:T(1024)S(1)}, f32[32,14,14,1024]{3,0,2,1:T(8,128)}) fusion(bf16[256,1024,1,1]{1,0,3,2:T(8,128)(2,1)S(1)} %bitcast.79, f32[32,14,14,256]{3,0,2,1:T(8,128)} %get-tuple-element.44, f32[256]{0:T(256)S(1)} %bitcast.92, f32[256]{0:T(256)S(1)} %bitcast.93, f32[256]{0:T(256)S(1)} %get-tuple-element.23, ...), kind=kOutput, calls=%fused_computation.1 | convolution fusion | flops 3317233664 | bytes 32649216 | tf_op jit(solution)/shard_map/dot_general | solution.py:41
  153.7 8.6 %all-reduce.1 = (f32[1024]{0:T(1024)S(1)}, f32[1024]{0:T(1024)S(1)}) all-reduce(f32[1024]{0:T(1024)S(1)} %get-tuple-element.8, f32[1024]{0:T(1024)S(1)} %get-tuple-element.7), channel_id=1, replica_groups=mesh['point'=8,'batch'=4] {'batch'}, use_global_device_ids=true, to_apply=%region_10.11 | all-reduce | flops 2048 | bytes 16384 | tf_op jit(solution)/shard_map/psum | solution.py:47
  162.9 14.7 %maximum_reduce_fusion = f32[32,1024]{1,0:T(8,128)S(1)} fusion(bf16[32,14,14,1024]{3,0,2,1:T(8,128)(2,1)} %param.11, f32[32,14,14,1024]{3,0,2,1:T(8,128)} %get-tuple-element.45, f32[1024]{0:T(1024)S(1)} %bitcast.82, f32[1024]{0:T(1024)S(1)} %bitcast.83, f32[1024]{0:T(1024)S(1)} %get-tuple-element.21, f32[1024]{0:T(1024)S(1)} %get-tuple-element.34), kind=kLoop, calls=%fused_computation | loop fusion | flops 51347456 | bytes 38682624 | tf_op jit(solution)/shard_map/reduce_sum | solution.py:114
  177.7 6.1 %select_reduce_fusion = (f32[32]{0:T(128)S(1)}, f32[32]{0:T(128)S(1)}) fusion(s32[32]{0:T(128)S(1)} %copy-done.6, f32[1000]{0:T(1024)S(1)} %bitcast.88, bf16[3,1000,1024]{2,1,0:T(8,128)(2,1)} %all-gather.8.cloned.1.call-done, f32[]{:T(128)} %bitcast.8, f32[]{:T(128)} %bitcast.6, f32[]{:T(128)} %bitcast.3, f32[32,1024]{1,0:T(8,128)S(1)} %maximum_reduce_fusion), kind=kOutput, calls=%fused_computation.31 | convolution fusion | flops 75009472 | bytes 6279468 | tf_op jit(solution)/shard_map/dot_general | solution.py:116
  185.1 39.5 %psum.55 = f32[8]{0:T(128)} all-reduce(f32[8]{0:T(128)S(1)} %compare_select_fusion), channel_id=1, replica_groups=mesh['point'=8,'batch'=4] {'point','batch'}, use_global_device_ids=true, to_apply=%region_17.18 | all-reduce | flops 8 | bytes 64 | tf_op jit(solution)/shard_map/psum | solution.py:130
  (35 shorter events, 5.1 us)
Async XLA Ops:
  7.2 31.0 %all-gather.10.cloned.1.call-start = ((), (), s32[]{:S(2)}) async-start(), calls=%async_computation.1 | async-start | bytes 1769472 | tf_op jit(solution)/shard_map/all_gather | solution.py:36
  7.9 57.8 %all-gather.14.cloned.1.call-start = ((), (), s32[]{:S(2)}) async-start(), calls=%async_computation.3 | async-start | bytes 1769472 | tf_op jit(solution)/shard_map/all_gather | solution.py:36
  8.7 92.8 %all-gather.12.cloned.1.call-start = ((), (), s32[]{:S(2)}) async-start(), calls=%async_computation.2 | async-start | bytes 3981312 | tf_op jit(solution)/shard_map/all_gather | solution.py:36
  9.4 168.3 %all-gather.8.cloned.1.call-start = ((), (), s32[]{:S(2)}) async-start(), calls=%async_computation | async-start | bytes 6912000 | tf_op jit(solution)/shard_map/all_gather | solution.py:34
  64.8 13.4 %copy-start.4 = (f32[256]{0:T(256)}, f32[256]{0:T(256)S(1)}, u32[]{:S(2)}) copy-start(f32[256]{0:T(256)S(1)} %get-tuple-element.39) | copy-start | bytes 3076
  101.4 6.2 %copy-start = (bf16[32,16,14,256]{3,0,2,1:T(8,128)(2,1)S(1)}, bf16[32,16,14,256]{3,0,2,1:T(8,128)(2,1)}, u32[]{:S(2)}) copy-start(bf16[32,16,14,256]{3,0,2,1:T(8,128)(2,1)} %get-tuple-element.27) | copy-start | bytes 11010052
  101.4 6.2 %copy-start.1 = (bf16[32,16,14,256]{3,0,2,1:T(8,128)(2,1)S(1)}, bf16[32,16,14,256]{3,0,2,1:T(8,128)(2,1)}, u32[]{:S(2)}) copy-start(bf16[32,16,14,256]{3,0,2,1:T(8,128)(2,1)} %get-tuple-element.28) | copy-start | bytes 11010052
  101.4 6.2 %copy-start.2 = (bf16[32,16,14,256]{3,0,2,1:T(8,128)(2,1)S(1)}, bf16[32,16,14,256]{3,0,2,1:T(8,128)(2,1)}, u32[]{:S(2)}) copy-start(bf16[32,16,14,256]{3,0,2,1:T(8,128)(2,1)} %get-tuple-element.29) | copy-start | bytes 11010052
  139.7 14.0 %copy-start.5 = (f32[256]{0:T(256)}, f32[256]{0:T(256)S(1)}, u32[]{:S(2)}) copy-start(f32[256]{0:T(256)S(1)} %get-tuple-element.38) | copy-start | bytes 3076
  162.9 14.8 %copy-start.3 = (f32[1024]{0:T(1024)}, f32[1024]{0:T(1024)S(1)}, u32[]{:S(2)}) copy-start(f32[1024]{0:T(1024)S(1)} %get-tuple-element.34) | copy-start | bytes 12292
  162.9 14.8 %copy-start.6 = (s32[32]{0:T(128)S(1)}, s32[32]{0:T(128)}, u32[]{:S(2)}) copy-start(s32[32]{0:T(128)} %param.12) | copy-start | bytes 388
Sparse Core Ops, SparseCore 0:
  9.9 28.2 all-gather.9
  40.1 25.5 all-gather.13
  67.6 33.8 all-gather.11
  103.2 45.9 all-gather.7
